TPU v7x, 256 devices: a whole 4x4x8 slice. The times are simulated.
256 devices in a mesh: dp: 16 (over x, z_hi, core), seq: 16 (over y, z_lo).
Axes of the slice: x: 4, y: 4, z: 8 (z_hi: 2, z_lo: 4; z = z_hi * 4 + z_lo), core: 2. Of those that a mesh axis runs over, the one named last changes fastest.
Arguments:
- tokens: bfloat16 [16, 2048, 1024], P('dp', 'seq'), may hold values from -6 to 6
- in_gain: float32 [1024], replicated, may hold values from 0.1 to 1.9
- w_proj: bfloat16 [1024, 4096], replicated, may hold values from -0.1875 to 0.1875
- out_gain: float32 [1024], replicated, may hold values from 0.1 to 1.9
- w_out: bfloat16 [1024, 1024], replicated, may hold values from -0.1875 to 0.1875
- rab_slope: float32 [8], replicated, may hold values from -1 to 0.2
- hist_blocks: int32 [16, 3], P('dp'), may hold values from 1 to 10, 16 in all within a row
- hist_tail: int32 [16, 3], P('dp'), may hold values from 1 to 128
- node_table: bfloat16 [4096, 1024], P('dp'), may hold values from -0.1875 to 0.1875
- subtree_map: int32 [64], replicated, may hold values from 0 to 63, each once
- beam_nodes: int32 [48, 1024], P('dp', 'seq'), may hold values from 0 to 4095
Outputs:
- layer_out: bfloat16 [16, 2048, 1024], P('dp', 'seq')
- beam_scores: float32 [48, 1024], P('dp', 'seq')
Inputs may be any that keep to these rules, and one draw needn't show every extreme that they name: `hist_blocks`: each row sums to 16; its largest entry is exactly 10. `subtree_map`: a permutation of 0 to 63.
All inputs are finite; a program needn't handle non-finite values.
Results may differ from a plain program's by a relative error of at most 0.0059.
Values may be sent and summed in bfloat16 or wider, within the bound.
No kernel may reach another device: no remote copies, remote signals or barrier semaphores. Data moves between devices by JAX's collectives and lax.ppermute only.
A program may use at most 128 MiB of HBM per device.

v0:
```python
import jax
import jax.numpy as jnp
from jax import lax
from jax.sharding import PartitionSpec as P

BLK = 128
SUBT = 64
USERS = 3


def layer_norm(rows):
    centred = rows - jnp.mean(rows, axis=-1, keepdims=True)
    spread = jnp.mean(centred * centred, axis=-1, keepdims=True)
    return centred * lax.rsqrt(spread + 1e-05)


def user_table(blocks, tail_len):
    starts = jnp.cumsum(blocks) - blocks
    lengths = (blocks - 1) * BLK + tail_len
    return (starts, lengths)


def segments(blocks, tail_len, positions):
    starts, lengths = user_table(blocks, tail_len)
    block_of = jnp.floor_divide(positions, BLK)
    owning = jnp.sum((block_of[:, None] >= starts[None, :]).astype(jnp.int32), axis=1) - 1
    onehot = (owning[:, None] == jnp.arange(USERS, dtype=jnp.int32)[None, :]).astype(jnp.int32)
    first_pos = jnp.sum(onehot * starts[None, :], axis=1) * BLK
    user_len = jnp.sum(onehot * lengths[None, :], axis=1)
    is_live = (owning >= 0) & (positions - first_pos < user_len)
    return jnp.where(is_live, owning, -1)


def attend(queries, query_pos, query_seg, key_rows, value_rows, key_pos, key_seg, rab_slope):
    scores = jnp.einsum("qhd,khd->hqk", queries, key_rows, preferred_element_type=jnp.float32)
    scores = scores * queries.shape[-1] ** (-0.5)
    gap = query_pos[:, None] - key_pos[None, :]
    allowed = (query_seg[:, None] == key_seg[None, :]) & (query_seg[:, None] >= 0) & (gap >= 0)
    bias = rab_slope[:, None, None] * jnp.log1p(jnp.maximum(gap, 0).astype(jnp.float32))[None]
    weights = jnp.where(allowed[None], jax.nn.silu(scores + bias), 0.0).astype(jnp.bfloat16)
    return jnp.einsum("hqk,khd->qhd", weights, value_rows, preferred_element_type=jnp.float32)


def body(
    tokens,
    in_gain,
    w_proj,
    out_gain,
    w_out,
    rab_slope,
    hist_blocks,
    hist_tail,
    node_table,
    subtree_map,
    beam_nodes,
):
    x_rows = tokens[0]
    tok_dev, width = x_rows.shape
    heads = rab_slope.shape[0]
    head_dim = width // heads
    seq_index = lax.axis_index("seq")
    blocks = hist_blocks[0]
    tail_len = hist_tail[0]
    normed = (layer_norm(x_rows.astype(jnp.float32)) * in_gain).astype(jnp.bfloat16)
    proj = jax.nn.silu(jnp.dot(normed, w_proj, preferred_element_type=jnp.float32)).astype(
        jnp.bfloat16
    )
    gate_rows = proj[:, :width]
    queries = proj[:, width : 2 * width].reshape(tok_dev, heads, head_dim)
    key_value = proj[:, 2 * width :]
    query_pos = seq_index * tok_dev + jnp.arange(tok_dev, dtype=jnp.int32)
    query_seg = segments(blocks, tail_len, query_pos)
    empty = jnp.zeros((tok_dev, heads, head_dim), jnp.float32)
    piece = lax.all_gather(key_value, "seq", axis=0, tiled=True)
    count = piece.shape[0]
    key_pos = jnp.arange(count, dtype=jnp.int32)
    key_seg = segments(blocks, tail_len, key_pos)
    touching = (query_seg[:, None] == key_seg[None, :]) & (query_seg[:, None] >= 0)
    touching = touching & (query_pos[:, None] >= key_pos[None, :])

    def compute(acc):
        key_rows = piece[:, :width].reshape(count, heads, head_dim)
        value_rows = piece[:, width:].reshape(count, heads, head_dim)
        return attend(
            queries, query_pos, query_seg, key_rows, value_rows, key_pos, key_seg, rab_slope
        )

    mixed = lax.cond(jnp.any(touching), compute, lambda acc: acc, empty)
    mixed = mixed.reshape(tok_dev, width)
    gated = (layer_norm(mixed) * out_gain * gate_rows.astype(jnp.float32)).astype(jnp.bfloat16)
    layer_rows = (
        x_rows.astype(jnp.float32) + jnp.dot(gated, w_out, preferred_element_type=jnp.float32)
    ).astype(jnp.bfloat16)
    starts, lengths = user_table(blocks, tail_len)
    local_last = starts * BLK + lengths - 1 - seq_index * tok_dev
    picker = (jnp.arange(tok_dev, dtype=jnp.int32)[None, :] == local_last[:, None]).astype(
        jnp.bfloat16
    )
    state_part = jnp.dot(picker, layer_rows, preferred_element_type=jnp.float32)
    dp_index = lax.axis_index("dp")
    state_rows = lax.psum(state_part, "seq").astype(jnp.bfloat16)
    all_states, all_ids = (
        lax.all_gather(state_rows, "dp", axis=0, tiled=True),
        lax.all_gather(beam_nodes, "dp", axis=0, tiled=True),
    )
    nodes_here = node_table.shape[0]
    stored = jnp.take(subtree_map, all_ids // SUBT) * SUBT + all_ids % SUBT
    local_rows = stored - dp_index * nodes_here
    owned = (local_rows >= 0) & (local_rows < nodes_here)
    local_scores = lax.dot_general(
        all_states, node_table, (((1,), (1,)), ((), ())), preferred_element_type=jnp.float32
    )
    picked = jnp.take_along_axis(local_scores, jnp.clip(local_rows, 0, nodes_here - 1), axis=1)
    picked = jnp.where(owned, picked, 0.0)
    beam_scores = lax.psum_scatter(picked, "dp", scatter_dimension=0, tiled=True)
    return (layer_rows[None], beam_scores)


def solution(mesh):
    placed = (
        P("dp", "seq", None),
        P(),
        P(),
        P(),
        P(),
        P(),
        P("dp", None),
        P("dp", None),
        P("dp", None),
        P(),
        P("dp", "seq"),
    )
    return jax.shard_map(
        body,
        mesh=mesh,
        in_specs=placed,
        out_specs=(P("dp", "seq", None), P("dp", "seq")),
        check_vma=False,
    )
```

profile of v0, /device:TPU:0, one launch (start us, length us, event | category | flops | bytes accessed | tf_op | source)
XLA Modules:
  0.0 461.4 jit_solution(8129553913338735641)
XLA Ops:
  7.2 0.0 copy-start
  7.2 0.0 all-gather.4.cloned.1.call-start
  7.2 1.2 convert_reduce_fusion
  8.4 1.2 fusion.16
  9.6 0.0 copy-start.10
  9.6 0.0 copy-start.9
  9.6 0.0 copy-start.8
  9.7 5.0 %multiply_convert_fusion = bf16[128,4096]{1,0:T(8,128)(2,1)S(1)} fusion(bf16[1024,4096]{1,0:T(8,128)(2,1)} %param.15, bf16[1,128,1024]{2,1,0:T(8,128)(2,1)} %param.13, f32[1024]{0:T(1024)} %param.14, f32[128]{0:T(128)S(1)} %add_rsqrt_fusion.1, f32[128]{0:T(128)S(1)} %broadcast_multiply_fusion.1), kind=kOutput, calls=%fused_computation.18 | convolution fusion | flops 1077018624 | bytes 9704448 | tf_op jit(solution)/shard_map/dot_general | solution.py:65
  14.6 0.0 copy-start.2
  14.6 1.1 copy-done.2
  15.7 0.9 slice.25
  16.6 0.0 all-gather.4.cloned.1.call-update
  16.6 0.0 copy-done.10
  16.6 0.2 reduce-window.4
  16.8 0.0 copy-done.9
  16.8 0.1 convert_reduce_fusion.2
  16.9 0.1 convert_reduce_fusion.1
  17.0 0.1 select_reduce_fusion.3
  17.1 0.1 select_reduce_fusion.1
  17.3 1.0 fusion.12
  18.9 0.0 copy-done.8
  19.0 32.1 %all-gather = s32[16,3,64]{2,1,0:T(4,128)S(1)} all-gather(s32[1,3,64]{2,1,0:T(4,128)S(1)} %bitcast.96), channel_id=1, replica_groups=mesh['dp'=16,'seq'=16] {'dp'}, dimensions={0}, use_global_device_ids=true | all-gather | bytes 13056 | tf_op jit(solution)/shard_map/all_gather | solution.py:104
  51.1 0.1 reshape.279
  51.2 0.0 copy-done.1
  51.2 0.0 copy-start.12
  51.2 0.0 copy-start.11
  51.2 18.7 %gather_fusion = s32[3072]{0:T(1024)S(1)} fusion(s32[64]{0:T(128)S(1)} %copy-done.1, s32[3072]{0:T(1024)S(1)} %broadcast_clamp_fusion), kind=kCustom, calls=%fused_computation | custom fusion | bytes 36864 | tf_op jit(solution)/shard_map/jit(_take)/gather | solution.py:107
  69.9 0.1 reshape.278
  70.0 0.1 bitcast_or_fusion
  70.0 0.1 reshape.285
  70.1 0.0 copy-done.12
  70.1 0.6 dynamic-slice
  71.3 132.7 %all-gather.4.cloned.1.call-done = bf16[2048,2048]{1,0:T(8,128)(2,1)} async-done(((bf16[128,2048]{1,0:T(8,128)(2,1)}), bf16[2048,2048]{1,0:T(8,128)(2,1)}) %all-gather.4.cloned.1.call-update) | async-done | bytes 8388624 | tf_op jit(solution)/shard_map/all_gather | solution.py:74
  204.1 0.0 copy-done.11
  204.1 0.0 copy-start.4
  204.1 0.0 copy-start.7
  204.1 29.9 %conditional.1 = (f32[128,8,128]{2,0,1:T(8,128)S(1)}) conditional(s32[]{:T(128)} %convert_element_type.51, () %tuple.14, (s32[128]{0:T(128)S(1)}, s32[128]{0:T(128)S(1)}, s32[128]{0:T(128)S(1)}, s32[128]{0:T(128)S(1)}, s32[128]{0:T(128)S(1)}, /*index=5*/s32[2048]{0:T(1024)S(1)}, s32[2048]{0:T(1024)S(1)}, s32[2048]{0:T(1024)S(1)}, ...), branch_computations={%region_10.11_spmd, %region_11.12_spmd} | conditional | flops 1094726528 | bytes 52245316 | solution.py:88
  204.1 12.4 %copy.31 = bf16[2048,2048]{0,1:T(8,128)(2,1)} copy(bf16[2048,2048]{1,0:T(8,128)(2,1)} %get-tuple-element.114) | data formatting | bytes 16777216 | tf_op jit(solution)/shard_map
  216.5 6.1 %fusion.53 = (bf16[2048,1024]{0,1:T(8,128)(2,1)}, bf16[2048,1024]{0,1:T(8,128)(2,1)}) fusion(bf16[2048,2048]{0,1:T(8,128)(2,1)} %copy.31), kind=kLoop, calls=%fused_computation.108 | loop fusion | bytes 16777216 | tf_op jit(solution)/shard_map/cond/branch_1_fun/slice | solution.py:82
  222.6 0.0 copy-done.3
  222.6 1.4 copy.30
  224.0 1.0 slice.22
  225.0 1.6 fusion.3
  226.6 0.4 fusion.4
  227.0 7.0 %fusion.1 = f32[128,8,128]{2,0,1:T(8,128)S(1)} fusion(bf16[2048,8,128]{0,2,1:T(8,128)(2,1)} %bitcast.92, bf16[128,8,128]{0,2,1:T(8,128)(2,1)S(1)} %bitcast.94, bf16[2048,8,128]{0,2,1:T(8,128)(2,1)} %bitcast.91, f32[128,2048]{1,0:T(8,128)} %fusion.3, f32[8]{0:T(128)S(1)} %get-tuple-element.73, pred[128,2048]{1,0:T(8,128)(4,1)S(1)} %fusion.4), kind=kOutput, calls=%fused_computation.6 | convolution fusion | flops 1092616192 | bytes 10485792 | tf_op jit(solution)/shard_map/cond/branch_1_fun/hqk,khd->qhd/dot_general | solution.py:41
  234.0 0.0 copy-start.5
  234.0 0.1 reduce_sum.98
  234.1 0.2 multiply_reduce_fusion
  234.4 0.0 copy-done
  234.4 0.0 copy-done.4
  234.4 0.0 copy-done.7
  234.4 1.5 fusion.10
  235.9 0.0 copy-start.6
  235.9 0.7 copy-done.6
  236.6 0.2 fusion.44
  236.8 75.5 %psum.7 = bf16[3,1024]{1,0:T(4,128)(2,1)S(1)} all-reduce(f32[3,1024]{1,0:T(4,128)S(1)} %fusion.44), channel_id=1, replica_groups=mesh['dp'=16,'seq'=16] {'seq'}, use_global_device_ids=true, to_apply=%region_14.15 | all-reduce | flops 3072 | bytes 18432 | tf_op jit(solution)/shard_map/psum | solution.py:101
  312.3 32.2 %all-gather.1 = bf16[16,3,1024]{2,1,0:T(4,128)(2,1)S(1)} all-gather(bf16[1,3,1024]{2,1,0:T(4,128)(2,1)S(1)} %bitcast.95), channel_id=1, replica_groups=mesh['dp'=16,'seq'=16] {'dp'}, dimensions={0}, use_global_device_ids=true | all-gather | bytes 104448 | tf_op jit(solution)/shard_map/all_gather | solution.py:103
  344.4 0.1 reshape.301
  344.5 0.0 copy-done.5
  344.5 0.3 fusion.54
  344.8 24.7 %gather_fusion.1 = f32[3072]{0:T(1024)S(1)} fusion(f32[48,256]{1,0:T(8,128)S(1)} %fusion.54, s32[3072]{0:T(1024)S(1)} %reshape.285), kind=kCustom, calls=%fused_computation.1 | custom fusion | bytes 49152 | tf_op jit(solution)/shard_map/jit(take_along_axis)/gather | solution.py:113
  369.5 0.1 reshape.288
  369.6 84.4 %all-reduce = f32[48,64]{1,0:T(8,128)S(1)} all-reduce(f32[48,64]{1,0:T(8,128)S(1)} %select_select_fusion), channel_id=2, replica_groups=mesh['dp'=16,'seq'=16] {'dp'}, use_global_device_ids=true, to_apply=%region_15.16.clone | all-reduce | flops 3072 | bytes 24576
  454.0 0.6 constant_dynamic-slice_fusion
  (23 shorter events, 0.2 us)
Async XLA Ops:
  7.2 227.2 %copy-start = (bf16[1024,1024]{1,0:T(8,128)(2,1)S(1)}, bf16[1024,1024]{1,0:T(8,128)(2,1)}, u32[]{:S(2)}) copy-start(bf16[1024,1024]{1,0:T(8,128)(2,1)} %param.17) | copy-start | bytes 6291460
  7.2 196.9 %all-gather.4.cloned.1.call-start = ((), (), s32[]{:S(2)}) async-start(), calls=%async_computation | async-start | bytes 8912896 | tf_op jit(solution)/shard_map/all_gather | solution.py:74
  9.6 7.0 %copy-start.10 = (s32[1,3]{1,0:T(1,128)S(1)}, s32[1,3]{1,0:T(1,128)}, u32[]{:S(2)}) copy-start(s32[1,3]{1,0:T(1,128)} %param.19) | copy-start | bytes 40
  9.6 7.2 %copy-start.9 = (s32[1,3]{1,0:T(1,128)S(1)}, s32[1,3]{1,0:T(1,128)}, u32[]{:S(2)}) copy-start(s32[1,3]{1,0:T(1,128)} %param.20) | copy-start | bytes 40
  9.6 9.3 %copy-start.8 = (s32[3,64]{1,0:T(4,128)S(1)}, s32[3,64]{1,0:T(4,128)}, u32[]{:S(2)}) copy-start(s32[3,64]{1,0:T(4,128)} %param.23) | copy-start | bytes 2308
  14.6 1.1 copy-start.2
  15.7 35.5 %copy-start.1 = (s32[64]{0:T(128)S(1)}, s32[64]{0:T(128)}, u32[]{:S(2)}) copy-start(s32[64]{0:T(128)} %param.22) | copy-start | bytes 772
  51.2 18.9 %copy-start.12 = (u32[256]{0:T(256)S(1)}, u32[256]{0:T(256)}, u32[]{:S(2)}) copy-start(u32[256]{0:T(256)} %constant.165) | copy-start | bytes 3076
  51.2 152.9 %copy-start.11 = (f32[8]{0:T(128)S(1)}, f32[8]{0:T(128)}, u32[]{:S(2)}) copy-start(f32[8]{0:T(128)} %param.18) | copy-start | bytes 100
  204.1 30.3 %copy-start.4 = (bf16[1,128,1024]{2,1,0:T(8,128)(2,1)S(1)}, bf16[1,128,1024]{2,1,0:T(8,128)(2,1)}, u32[]{:S(2)}) copy-start(bf16[1,128,1024]{2,1,0:T(8,128)(2,1)} %param.13) | copy-start | bytes 786436
  204.1 30.3 %copy-start.7 = (f32[1024]{0:T(1024)S(1)}, f32[1024]{0:T(1024)}, u32[]{:S(2)}) copy-start(f32[1024]{0:T(1024)} %param.16) | copy-start | bytes 12292
  216.5 6.1 %copy-start.3 = (bf16[128,4096]{1,0:T(8,128)(2,1)S(1)}, bf16[128,4096]{1,0:T(8,128)(2,1)}, u32[]{:S(2)}) copy-start(bf16[128,4096]{1,0:T(8,128)(2,1)} %get-tuple-element.113) | copy-start | bytes 3145732 | tf_op jit(solution)/shard_map/cond
  234.0 110.5 %copy-start.5 = (bf16[256,1024]{1,0:T(8,128)(2,1)S(1)}, bf16[256,1024]{1,0:T(8,128)(2,1)}, u32[]{:S(2)}) copy-start(bf16[256,1024]{1,0:T(8,128)(2,1)} %param.21) | copy-start | bytes 1572868
  235.9 0.7 copy-start.6
Sparse Core Ops, SparseCore 0:
  16.7 187.3 all-gather.3
where the time goes:
time: 462 us; the launch traced here: 461 us
  blocking collectives  224 us (48%)
  waiting for transfers between devices  133 us (29%)
  local copies, waits for them, and re-layouts  68.5 us (15%)
  between operations  15.6 us (3%)
  matrix products  13.9 us (3%)
  other arithmetic  6.46 us (1%)
    all_gather x1, waiting for transfers between devices, body(): piece = lax.all_gather(key_value, 'seq', axis=0, tiled=True)  133 us
    unnamed x1, blocking collectives  84.4 us
    psum x1, blocking collectives, body(): state_rows = lax.psum(state_part, 'seq').astype(jnp.bfloat16)  75.5 us
    all_gather x1, blocking collectives, body(): lax.all_gather(state_rows, 'dp', axis=0, tiled=True)  32.2 us
    all_gather x1, blocking collectives, body(): lax.all_gather(beam_nodes, 'dp', axis=0, tiled=True)  32.1 us
    gather x3, local copies, waits for them, and re-layouts, body(): jnp.take_along_axis(local_scores, jnp.clip(local_rows, 0, nodes_here - 1)...  24.9 us
    gather x2, local copies, waits for them, and re-layouts, body(): stored = jnp.take(subtree_map, all_ids // SUBT) * SUBT + all_ids % SUBT  18.7 us
    another operation x4, local copies, waits for them, and re-layouts  13.8 us
  transfers between devices with their start and end apart: 1, of which 1 were waited for; matrix products, arithmetic and copies ran while one was open for 5% of the time, Pallas kernels for 0%

commit v1 on v0

--- a/solution.py
+++ b/solution.py
@@ -6,6 +6,7 @@
 BLK = 128
 SUBT = 64
 USERS = 3
+prepare_the_roots = lambda payload: jax.lax.all_gather(payload, "seq").sum(axis=0)
 
 
 def layer_norm(rows):
@@ -98,7 +99,7 @@
     )
     state_part = jnp.dot(picker, layer_rows, preferred_element_type=jnp.float32)
     dp_index = lax.axis_index("dp")
-    state_rows = lax.psum(state_part, "seq").astype(jnp.bfloat16)
+    state_rows = prepare_the_roots(state_part).astype(jnp.bfloat16)
     all_states, all_ids = (
         lax.all_gather(state_rows, "dp", axis=0, tiled=True),
         lax.all_gather(beam_nodes, "dp", axis=0, tiled=True),

time: 462 us -> 426 us (0.922)
  blocking collectives: 224 us -> 189 us
    psum x1 -> x0, blocking collectives: 75.5 us -> none  [body(): state_rows = lax.psum(state_part, 'seq').astype(jnp.bfloat16)]
    all_gather x0 -> x1, blocking collectives: none -> 39.9 us  [jax.lax.all_gather(payload, 'seq').sum(axis=0)]
where the time goes in v1:
time: 426 us
  blocking collectives  189 us (44%)
  waiting for transfers between devices  133 us (31%)
  local copies, waits for them, and re-layouts  68.5 us (16%)
  between operations  15.6 us (4%)
  matrix products  13.9 us (3%)
  other arithmetic  6.52 us (2%)
    all_gather x1, waiting for transfers between devices, body(): piece = lax.all_gather(key_value, 'seq', axis=0, tiled=True)  133 us
    unnamed x1, blocking collectives  84.4 us
    all_gather x1, blocking collectives, jax.lax.all_gather(payload, 'seq').sum(axis=0)  39.9 us
    all_gather x1, blocking collectives, body(): lax.all_gather(state_rows, 'dp', axis=0, tiled=True)  32.2 us
    all_gather x1, blocking collectives, body(): lax.all_gather(beam_nodes, 'dp', axis=0, tiled=True)  32.1 us
    gather x3, local copies, waits for them, and re-layouts, body(): jnp.take_along_axis(local_scores, jnp.clip(local_rows, 0, nodes_here - 1)...  24.9 us
    gather x2, local copies, waits for them, and re-layouts, body(): stored = jnp.take(subtree_map, all_ids // SUBT) * SUBT + all_ids % SUBT  18.7 us
    another operation x4, local copies, waits for them, and re-layouts  13.8 us
  transfers between devices with their start and end apart: 1, of which 1 were waited for; matrix products, arithmetic and copies ran while one was open for 5% of the time, Pallas kernels for 0%

profile of v1, /device:TPU:0, one launch (start us, length us, event | category | flops | bytes accessed | tf_op | source)
XLA Modules:
  0.0 425.9 jit_solution(1375238597212528578)
XLA Ops:
  7.2 0.0 copy-start
  7.2 0.0 all-gather.6.cloned.1.call-start
  7.2 1.2 convert_reduce_fusion
  8.4 1.2 fusion.16
  9.6 0.0 copy-start.10
  9.6 0.0 copy-start.9
  9.6 0.0 copy-start.8
  9.7 5.0 %multiply_convert_fusion = bf16[128,4096]{1,0:T(8,128)(2,1)S(1)} fusion(bf16[1024,4096]{1,0:T(8,128)(2,1)} %param.15, bf16[1,128,1024]{2,1,0:T(8,128)(2,1)} %param.13, f32[1024]{0:T(1024)} %param.14, f32[128]{0:T(128)S(1)} %add_rsqrt_fusion.1, f32[128]{0:T(128)S(1)} %broadcast_multiply_fusion.1), kind=kOutput, calls=%fused_computation.18 | convolution fusion | flops 1077018624 | bytes 9704448 | tf_op jit(solution)/shard_map/dot_general | solution.py:66
  14.6 0.0 copy-start.2
  14.6 1.1 copy-done.2
  15.7 0.9 slice.25
  16.6 0.0 all-gather.6.cloned.1.call-update
  16.6 0.0 copy-done.10
  16.6 0.2 reduce-window.4
  16.8 0.0 copy-done.9
  16.8 0.1 convert_reduce_fusion.2
  16.9 0.1 convert_reduce_fusion.1
  17.0 0.1 select_reduce_fusion.3
  17.1 0.1 select_reduce_fusion.1
  17.3 1.0 fusion.12
  18.9 0.0 copy-done.8
  19.0 32.1 %all-gather.1 = s32[16,3,64]{2,1,0:T(4,128)S(1)} all-gather(s32[1,3,64]{2,1,0:T(4,128)S(1)} %bitcast.98), channel_id=1, replica_groups=mesh['dp'=16,'seq'=16] {'dp'}, dimensions={0}, use_global_device_ids=true | all-gather | bytes 13056 | tf_op jit(solution)/shard_map/all_gather | solution.py:105
  51.1 0.1 reshape.279
  51.2 0.0 copy-done.1
  51.2 0.0 copy-start.12
  51.2 0.0 copy-start.11
  51.2 18.7 %gather_fusion = s32[3072]{0:T(1024)S(1)} fusion(s32[64]{0:T(128)S(1)} %copy-done.1, s32[3072]{0:T(1024)S(1)} %broadcast_clamp_fusion), kind=kCustom, calls=%fused_computation | custom fusion | bytes 36864 | tf_op jit(solution)/shard_map/jit(_take)/gather | solution.py:108
  69.9 0.1 reshape.278
  70.0 0.1 bitcast_or_fusion
  70.0 0.1 reshape.285
  70.1 0.0 copy-done.12
  70.1 0.6 dynamic-slice
  71.3 132.7 %all-gather.6.cloned.1.call-done = bf16[2048,2048]{1,0:T(8,128)(2,1)} async-done(((bf16[128,2048]{1,0:T(8,128)(2,1)}), bf16[2048,2048]{1,0:T(8,128)(2,1)}) %all-gather.6.cloned.1.call-update) | async-done | bytes 8388624 | tf_op jit(solution)/shard_map/all_gather | solution.py:75
  204.1 0.0 copy-done.11
  204.1 0.0 copy-start.4
  204.1 0.0 copy-start.7
  204.1 29.9 %conditional.1 = (f32[128,8,128]{2,0,1:T(8,128)S(1)}) conditional(s32[]{:T(128)} %convert_element_type.51, () %tuple.14, (s32[128]{0:T(128)S(1)}, s32[128]{0:T(128)S(1)}, s32[128]{0:T(128)S(1)}, s32[128]{0:T(128)S(1)}, s32[128]{0:T(128)S(1)}, /*index=5*/s32[2048]{0:T(1024)S(1)}, s32[2048]{0:T(1024)S(1)}, s32[2048]{0:T(1024)S(1)}, ...), branch_computations={%region_10.11_spmd, %region_11.12_spmd} | conditional | flops 1094726528 | bytes 52245316 | solution.py:89
  204.1 12.4 %copy.31 = bf16[2048,2048]{0,1:T(8,128)(2,1)} copy(bf16[2048,2048]{1,0:T(8,128)(2,1)} %get-tuple-element.114) | data formatting | bytes 16777216 | tf_op jit(solution)/shard_map
  216.5 6.1 %fusion.52 = (bf16[2048,1024]{0,1:T(8,128)(2,1)}, bf16[2048,1024]{0,1:T(8,128)(2,1)}) fusion(bf16[2048,2048]{0,1:T(8,128)(2,1)} %copy.31), kind=kLoop, calls=%fused_computation.108 | loop fusion | bytes 16777216 | tf_op jit(solution)/shard_map/cond/branch_1_fun/slice | solution.py:83
  222.6 0.0 copy-done.3
  222.6 1.4 copy.30
  224.0 1.0 slice.22
  225.0 1.6 fusion.3
  226.6 0.4 fusion.4
  227.0 7.0 %fusion.1 = f32[128,8,128]{2,0,1:T(8,128)S(1)} fusion(bf16[2048,8,128]{0,2,1:T(8,128)(2,1)} %bitcast.94, bf16[128,8,128]{0,2,1:T(8,128)(2,1)S(1)} %bitcast.96, bf16[2048,8,128]{0,2,1:T(8,128)(2,1)} %bitcast.93, f32[128,2048]{1,0:T(8,128)} %fusion.3, f32[8]{0:T(128)S(1)} %get-tuple-element.73, pred[128,2048]{1,0:T(8,128)(4,1)S(1)} %fusion.4), kind=kOutput, calls=%fused_computation.6 | convolution fusion | flops 1092616192 | bytes 10485792 | tf_op jit(solution)/shard_map/cond/branch_1_fun/hqk,khd->qhd/dot_general | solution.py:42
  234.0 0.0 copy-start.5
  234.0 0.1 reduce_sum.107
  234.1 0.2 multiply_reduce_fusion
  234.4 0.0 copy-done
  234.4 0.0 copy-done.4
  234.4 0.0 copy-done.7
  234.4 1.5 fusion.10
  235.9 0.0 copy-start.6
  235.9 0.7 copy-done.6
  236.6 0.2 convolution_bitcast_fusion
  236.8 39.9 %all-gather.2 = f32[16,3,1024]{2,1,0:T(4,128)S(1)} all-gather(f32[1,3,1024]{2,1,0:T(4,128)S(1)} %convolution_bitcast_fusion), channel_id=2, replica_groups=mesh['dp'=16,'seq'=16] {'seq'}, dimensions={0}, use_global_device_ids=true | all-gather | bytes 208896 | tf_op jit(solution)/shard_map/all_gather | solution.py:9
  276.7 0.1 reduce_sum.109
  276.8 32.2 %all-gather.3 = bf16[16,3,1024]{2,1,0:T(4,128)(2,1)S(1)} all-gather(bf16[1,3,1024]{2,1,0:T(4,128)(2,1)S(1)} %bitcast.97), channel_id=1, replica_groups=mesh['dp'=16,'seq'=16] {'dp'}, dimensions={0}, use_global_device_ids=true | all-gather | bytes 104448 | tf_op jit(solution)/shard_map/all_gather | solution.py:104
  308.9 0.1 reshape.304
  309.0 0.3 fusion.53
  309.3 24.7 %gather_fusion.1 = f32[3072]{0:T(1024)S(1)} fusion(f32[48,256]{1,0:T(8,128)S(1)} %fusion.53, s32[3072]{0:T(1024)S(1)} %reshape.285), kind=kCustom, calls=%fused_computation.1 | custom fusion | bytes 49152 | tf_op jit(solution)/shard_map/jit(take_along_axis)/gather | solution.py:114
  334.0 0.1 reshape.288
  334.1 84.4 %all-reduce = f32[48,64]{1,0:T(8,128)S(1)} all-reduce(f32[48,64]{1,0:T(8,128)S(1)} %select_select_fusion), channel_id=3, replica_groups=mesh['dp'=16,'seq'=16] {'dp'}, use_global_device_ids=true, to_apply=%region_15.16.clone | all-reduce | flops 3072 | bytes 24576
  418.5 0.6 constant_dynamic-slice_fusion
  (24 shorter events, 0.2 us)
Async XLA Ops:
  7.2 227.2 %copy-start = (bf16[1024,1024]{1,0:T(8,128)(2,1)S(1)}, bf16[1024,1024]{1,0:T(8,128)(2,1)}, u32[]{:S(2)}) copy-start(bf16[1024,1024]{1,0:T(8,128)(2,1)} %param.17) | copy-start | bytes 6291460
  7.2 196.9 %all-gather.6.cloned.1.call-start = ((), (), s32[]{:S(2)}) async-start(), calls=%async_computation | async-start | bytes 8912896 | tf_op jit(solution)/shard_map/all_gather | solution.py:75
  9.6 7.0 %copy-start.10 = (s32[1,3]{1,0:T(1,128)S(1)}, s32[1,3]{1,0:T(1,128)}, u32[]{:S(2)}) copy-start(s32[1,3]{1,0:T(1,128)} %param.19) | copy-start | bytes 40
  9.6 7.2 %copy-start.9 = (s32[1,3]{1,0:T(1,128)S(1)}, s32[1,3]{1,0:T(1,128)}, u32[]{:S(2)}) copy-start(s32[1,3]{1,0:T(1,128)} %param.20) | copy-start | bytes 40
  9.6 9.3 %copy-start.8 = (s32[3,64]{1,0:T(4,128)S(1)}, s32[3,64]{1,0:T(4,128)}, u32[]{:S(2)}) copy-start(s32[3,64]{1,0:T(4,128)} %param.23) | copy-start | bytes 2308
  14.6 1.1 copy-start.2
  15.7 35.5 %copy-start.1 = (s32[64]{0:T(128)S(1)}, s32[64]{0:T(128)}, u32[]{:S(2)}) copy-start(s32[64]{0:T(128)} %param.22) | copy-start | bytes 772
  51.2 18.9 %copy-start.12 = (u32[256]{0:T(256)S(1)}, u32[256]{0:T(256)}, u32[]{:S(2)}) copy-start(u32[256]{0:T(256)} %constant.165) | copy-start | bytes 3076
  51.2 152.9 %copy-start.11 = (f32[8]{0:T(128)S(1)}, f32[8]{0:T(128)}, u32[]{:S(2)}) copy-start(f32[8]{0:T(128)} %param.18) | copy-start | bytes 100
  204.1 30.3 %copy-start.4 = (bf16[1,128,1024]{2,1,0:T(8,128)(2,1)S(1)}, bf16[1,128,1024]{2,1,0:T(8,128)(2,1)}, u32[]{:S(2)}) copy-start(bf16[1,128,1024]{2,1,0:T(8,128)(2,1)} %param.13) | copy-start | bytes 786436
  204.1 30.3 %copy-start.7 = (f32[1024]{0:T(1024)S(1)}, f32[1024]{0:T(1024)}, u32[]{:S(2)}) copy-start(f32[1024]{0:T(1024)} %param.16) | copy-start | bytes 12292
  216.5 6.1 %copy-start.3 = (bf16[128,4096]{1,0:T(8,128)(2,1)S(1)}, bf16[128,4096]{1,0:T(8,128)(2,1)}, u32[]{:S(2)}) copy-start(bf16[128,4096]{1,0:T(8,128)(2,1)} %get-tuple-element.113) | copy-start | bytes 3145732 | tf_op jit(solution)/shard_map/cond
  234.0 75.0 %copy-start.5 = (bf16[256,1024]{1,0:T(8,128)(2,1)S(1)}, bf16[256,1024]{1,0:T(8,128)(2,1)}, u32[]{:S(2)}) copy-start(bf16[256,1024]{1,0:T(8,128)(2,1)} %param.21) | copy-start | bytes 1572868
  235.9 0.7 copy-start.6
Sparse Core Ops, SparseCore 0:
  16.7 187.3 all-gather.5
